TPU v7x, 256 devices: a whole 4x4x8 slice. The times are simulated.
256 devices in a mesh: gx: 2 (over core), gy: 4 (over x), gz: 32 (over z, y).
Axes of the slice: x: 4, y: 4, z: 8, core: 2. Of those that a mesh axis runs over, the one named last changes fastest.
Arguments:
- resid_x: float32 [6, 8, 32, 120, 512], P('gx', 'gy', 'gz'), may hold values from -6 to 6
- resid_y: float32 [4, 12, 32, 120, 512], P('gx', 'gy', 'gz'), may hold values from -6 to 6
- face_weights: float32 [4, 8, 32, 4, 120], P('gx', 'gy', 'gz'), may hold values from 0.25 to 0.75
- face_counts: int32 [4, 8, 32, 4], P('gx', 'gy', 'gz'), may hold values from 1 to 4, as said below
- neumann: bfloat16 [4, 8, 32, 480, 480], P('gx', 'gy', 'gz'), may hold values from -0.25 to 0.25
- schur: bfloat16 [4, 8, 32, 480, 480], P('gx', 'gy', 'gz'), may hold values from -0.25 to 0.25
- basis: bfloat16 [4, 8, 32, 480, 64], P('gx', 'gy', 'gz'), may hold values from -0.25 to 0.25
- coarse_map: int32 [4, 8, 32, 64], P('gx', 'gy', 'gz'), may hold values from 0 to 511
- column_inverse: float32 [2, 4, 512, 512], P('gx', 'gy', 'gz'), may hold values from -0.25 to 0.25
- column_basis: float32 [2, 4, 512, 512], P('gx', 'gy', 'gz'), may hold values from -0.25 to 0.25
- top_inverse: float32 [512, 512], replicated, may hold values from -0.09375 to 0.09375
Outputs:
- z_x: float32 [6, 8, 32, 120, 512], P('gx', 'gy', 'gz')
- z_y: float32 [4, 12, 32, 120, 512], P('gx', 'gy', 'gz')
- schur_image: bfloat16 [4, 8, 32, 480, 512], P('gx', 'gy', 'gz')
Inputs may be any that keep to these rules, and one draw needn't show every extreme that they name: `face_counts`: only the first 30 * count of a face's 120 dofs are live; about one face in eight has 4 live mesh faces. `coarse_map`: several local coarse dofs may share a column coarse dof.
All inputs are finite; a program needn't handle non-finite values.
Results may differ from a plain program's by a relative error of at most 0.0063.
Values sent between devices are 32-bit elements; how exact they have to be, the bound alone decides.
No kernel may reach another device: no remote copies, remote signals or barrier semaphores. Data moves between devices by JAX's collectives and lax.ppermute only.
A program may use at most 64 MiB of HBM per device.

v0:
```python
import jax
import jax.numpy as jnp
from jax import lax
from jax.sharding import PartitionSpec as P

BLK = 30


def with_halo(array, sides, width):
    for axis, dim in sides:
        size, length = (lax.axis_size(axis), array.shape[dim])
        up = [(i, (i + 1) % size) for i in range(size)]
        down = [(j, i) for i, j in up]
        last = lax.slice_in_dim(array, length - width, length, axis=dim)
        initial = lax.slice_in_dim(array, 0, width, axis=dim)
        before = lax.ppermute(last, axis, up)
        after = lax.ppermute(initial, axis, down)
        array = jnp.concatenate([before, array, after], axis=dim)
    return array


def assemble_x(copies):
    padded = with_halo(copies, (("gx", 0),), 1)
    return copies + jnp.stack([padded[0], jnp.zeros_like(padded[0]), padded[4]], 0)


def assemble_y(copies):
    padded = with_halo(copies, (("gy", 1),), 1)
    return copies + jnp.stack([padded[:, 0], jnp.zeros_like(padded[:, 0]), padded[:, 4]], 1)


def gather_faces(along_x, along_y):
    return jnp.stack([along_x[0:2], along_x[1:3], along_y[:, 0:2], along_y[:, 1:3]], 2)


def on_device(
    resid_x,
    resid_y,
    face_weights,
    face_counts,
    neumann,
    schur,
    basis,
    coarse_map,
    column_inverse,
    column_basis,
    top_inverse,
):
    high = lax.Precision.HIGHEST
    face_dofs = resid_x.shape[3]
    loads = resid_x.shape[4]
    inner = neumann.shape[3]
    coarse_local = basis.shape[4]
    column_size = column_inverse.shape[3]
    dof_index = jnp.arange(face_dofs, dtype=jnp.int32)
    live = (dof_index[None, None, None, :] < face_counts[:, :, 0, :, None] * BLK).astype(
        jnp.float32
    )
    scale = face_weights[:, :, 0] * live
    assembled_x = assemble_x(resid_x)[:, :, 0]
    assembled_y = assemble_y(resid_y)[:, :, 0]
    faces = gather_faces(assembled_x, assembled_y)
    upart = (faces * scale[..., None]).reshape(4, inner, loads).astype(jnp.bfloat16)
    neumann_flat = neumann.reshape(4, inner, inner)
    basis_flat = basis.reshape(4, inner, coarse_local)
    wpart = jnp.einsum("snk,skr->snr", neumann_flat, upart, preferred_element_type=jnp.float32)
    gpart = jnp.einsum("snc,snr->scr", basis_flat, upart, preferred_element_type=jnp.float32)
    targets = coarse_map.reshape(4 * coarse_local)
    onehot = (targets[:, None] == jnp.arange(column_size, dtype=jnp.int32)[None, :]).astype(
        jnp.float32
    )
    column_part = lax.dot_general(
        onehot, gpart.reshape(4 * coarse_local, loads), (((0,), (0,)), ((), ())), precision=high
    )
    column_res = lax.psum(column_part, "gz")
    inverse_rows = column_inverse[0, 0]
    basis_rows = column_basis[0, 0]
    row_count = inverse_rows.shape[0]
    row_start = lax.axis_index("gz") * row_count
    own_rows = lax.dynamic_slice_in_dim(column_res, row_start, row_count, 0)
    level_two = jnp.dot(inverse_rows, column_res, precision=high)
    top_part = lax.dot_general(basis_rows, own_rows, (((0,), (0,)), ((), ())), precision=high)
    column_top = lax.psum(top_part, "gz")
    top_res = lax.psum(column_top, ("gx", "gy"))
    level_three = jnp.dot(top_inverse, top_res, precision=high)
    value_rows = level_two + jnp.dot(basis_rows, level_three, precision=high)
    column_vals = lax.all_gather(value_rows, "gz", axis=0, tiled=True)
    coarse_vals = (
        jnp.dot(onehot, column_vals, precision=high)
        .reshape(4, coarse_local, loads)
        .astype(jnp.bfloat16)
    )
    ypart = wpart + jnp.einsum(
        "snc,scr->snr", basis_flat, coarse_vals, preferred_element_type=jnp.float32
    )
    contrib = ypart.reshape(2, 2, 4, face_dofs, loads) * scale[..., None]
    send_x = jnp.stack(
        [contrib[0, :, 0], contrib[0, :, 1] + contrib[1, :, 0], contrib[1, :, 1]], 0
    )[:, :, None]
    send_y = jnp.stack(
        [contrib[:, 0, 2], contrib[:, 0, 3] + contrib[:, 1, 2], contrib[:, 1, 3]], 1
    )[:, :, None]
    z_x = assemble_x(send_x)
    z_y = assemble_y(send_y)
    zfaces = gather_faces(z_x[:, :, 0], z_y[:, :, 0])
    zsub = (zfaces * live[..., None]).reshape(4, inner, loads).astype(jnp.bfloat16)
    image = jnp.einsum(
        "snk,skr->snr", schur.reshape(4, inner, inner), zsub, preferred_element_type=jnp.float32
    )
    return (z_x, z_y, image.astype(jnp.bfloat16).reshape(2, 2, 1, inner, loads))


def solution(mesh):
    return jax.shard_map(
        on_device,
        mesh=mesh,
        in_specs=(
            P("gx", "gy", "gz", None, None),
            P("gx", "gy", "gz", None, None),
            P("gx", "gy", "gz", None, None),
            P("gx", "gy", "gz", None),
            P("gx", "gy", "gz", None, None),
            P("gx", "gy", "gz", None, None),
            P("gx", "gy", "gz", None, None),
            P("gx", "gy", "gz", None),
            P("gx", "gy", "gz", None),
            P("gx", "gy", "gz", None),
            P(),
        ),
        out_specs=(
            P("gx", "gy", "gz", None, None),
            P("gx", "gy", "gz", None, None),
            P("gx", "gy", "gz", None, None),
        ),
        check_vma=False,
    )
```

profile of v0, /device:TPU:6, one launch (start us, length us, event | category | flops | bytes accessed | tf_op | source)
XLA Modules:
  0.0 522.4 jit_solution(4546723145671781828)
XLA Ops:
  7.2 2.4 fusion.25
  9.6 2.2 collective-permute-start.2
  11.9 0.8 copy.74
  12.7 0.8 copy.75
  13.5 0.5 collective-permute-start
  14.0 0.6 broadcast.80
  14.6 0.6 reduce.3
  15.8 7.1 %collective-permute-done.2 = f32[2,1,1,120,512]{4,3,1,0,2:T(8,128)} collective-permute-done((f32[2,1,1,120,512]{4,3,1,0,2:T(8,128)}, f32[2,1,1,120,512]{4,3,1,0,2:T(8,128)}, u32[]{:S(2)}, u32[]{:S(2)}) %collective-permute-start.2) | collective-permute-done | bytes 491552 | tf_op jit(solution)/shard_map/ppermute | solution.py:16
  22.9 1.2 collective-permute-done.3
  24.1 1.5 fusion.3
  25.6 0.2 slice_bitcast_fusion.3
  25.9 1.1 copy-done.6
  27.0 1.5 maximum_add_fusion
  28.5 0.2 fusion.23
  28.7 0.6 pad_maximum_fusion
  29.3 0.3 copy-done.9
  29.7 0.5 fusion.7
  30.2 1.0 copy-done.2
  31.2 1.7 fusion.8
  33.0 153.5 %all-reduce.4.cloned.1.call-done = f32[512,512]{1,0:T(8,128)} async-done(((f32[512,512]{1,0:T(8,128)}), f32[512,512]{1,0:T(8,128)}) %all-reduce.4.cloned.1.call-update) | async-done | bytes 1048592 | tf_op jit(solution)/shard_map/psum | solution.py:75
  186.5 2.8 convolution_bitcast_fusion
  189.4 148.8 %all-reduce.6.cloned.1.call-done = f32[512,512]{0,1:T(8,128)} async-done(((f32[512,512]{0,1:T(8,128)}), f32[512,512]{0,1:T(8,128)}) %all-reduce.6.cloned.1.call-update) | async-done | bytes 1048592 | tf_op jit(solution)/shard_map/psum | solution.py:83
  338.5 0.7 fusion.15
  339.2 64.1 %all-reduce.8.cloned.1.call-done = f32[512,512]{0,1:T(8,128)} async-done(((f32[512,512]{0,1:T(8,128)}), f32[512,512]{0,1:T(8,128)}) %all-reduce.8.cloned.1.call-update) | async-done | bytes 1048592 | tf_op jit(solution)/shard_map/psum | solution.py:84
  403.3 3.4 fusion.26
  406.7 1.6 fusion.5
  408.4 78.2 %all-gather.2.cloned.1.call-done = f32[512,512]{1,0:T(8,128)} async-done(((f32[16,512]{1,0:T(8,128)}), f32[512,512]{1,0:T(8,128)}) %all-gather.2.cloned.1.call-update) | async-done | bytes 1048592 | tf_op jit(solution)/shard_map/all_gather | solution.py:87
  486.6 2.0 convolution_convert_fusion
  488.6 0.7 fusion.27
  489.3 1.4 copy-done.3
  490.7 1.3 convolution_add_fusion
  492.0 0.3 copy_multiply_fusion
  492.6 0.5 collective-permute-start.4
  493.1 0.4 slice_bitcast_fusion.6
  493.7 0.6 collective-permute-start.6
  494.4 1.5 collective-permute-start.7
  495.9 0.3 maximum_add_fusion.2
  496.2 1.3 copy.68
  497.6 9.4 %collective-permute-done.6 = f32[2,1,1,120,512]{4,3,0,2,1:T(8,128)S(1)} collective-permute-done((f32[2,1,1,120,512]{4,3,0,2,1:T(8,128)S(1)}, f32[2,1,1,120,512]{4,3,0,2,1:T(8,128)S(1)}, u32[]{:S(2)}, u32[]{:S(2)}) %collective-permute-start.6) | collective-permute-done | bytes 491552 | tf_op jit(solution)/shard_map/ppermute | solution.py:16
  507.0 1.5 collective-permute-done.7
  508.6 0.3 maximum_add_fusion.4
  508.9 0.2 slice_bitcast_fusion.1
  509.2 0.6 pad_maximum_fusion.1
  509.7 0.6 copy.67
  510.3 1.0 copy-done.7
  511.3 2.5 fusion.2
  513.8 1.5 fusion.4
  515.3 0.6 copy-done.1
  (56 shorter events, 1.8 us)
Async XLA Ops:
  7.2 482.1 %copy-start = (bf16[2,2,1,480,480]{4,3,2,1,0:T(8,128)(2,1)S(1)}, bf16[2,2,1,480,480]{4,3,2,1,0:T(8,128)(2,1)}, u32[]{:S(2)}) copy-start(bf16[2,2,1,480,480]{4,3,2,1,0:T(8,128)(2,1)} %param.15) | copy-start | bytes 5529604
  7.2 4.6 copy-start.5
  7.2 179.3 %all-reduce.4.cloned.1.call-start = ((), (), s32[]{:S(2)}) async-start(), calls=%async_computation | async-start | bytes 2097152 | tf_op jit(solution)/shard_map/psum | solution.py:75
  9.6 13.3 %collective-permute-start.2 = (f32[2,1,1,120,512]{4,3,1,0,2:T(8,128)}, f32[2,1,1,120,512]{4,3,1,0,2:T(8,128)}, u32[]{:S(2)}, u32[]{:S(2)}) collective-permute-start(f32[2,1,1,120,512]{4,3,1,0,2:T(8,128)} %get-tuple-element.35), channel_id=1, source_target_pairs={{0,32},{32,64},{64,96},{96,0},{1,33},{33,65},{65,97},{97,1},{2,34}... | collective-permute-start | bytes 1474568 | tf_op jit(solution)/shard_map/ppermute | solution.py:16
  11.8 12.3 %collective-permute-start.3 = (f32[2,1,1,120,512]{4,3,1,0,2:T(8,128)}, f32[2,1,1,120,512]{4,3,1,0,2:T(8,128)}, u32[]{:S(2)}, u32[]{:S(2)}) collective-permute-start(f32[2,1,1,120,512]{4,3,1,0,2:T(8,128)} %get-tuple-element.36), channel_id=1, source_target_pairs={{32,0},{64,32},{96,64},{0,96},{33,1},{65,33},{97,65},{1,97},{34,2}... | collective-permute-start | bytes 1474568 | tf_op jit(solution)/shard_map/ppermute | solution.py:17
  11.9 2.2 copy-start.13
  11.9 2.7 copy-start.14
  11.9 3.7 copy-start.12
  11.9 12.2 %copy-start.4 = (f32[2,3,1,120,512]{4,3,2,1,0:T(8,128)S(1)}, f32[2,3,1,120,512]{4,3,2,1,0:T(8,128)}, u32[]{:S(2)}) copy-start(f32[2,3,1,120,512]{4,3,2,1,0:T(8,128)} %param.12) | copy-start | bytes 4423684
  12.7 13.1 %collective-permute-start.1 = (f32[1,2,1,120,512]{4,3,0,1,2:T(8,128)}, f32[1,2,1,120,512]{4,3,0,1,2:T(8,128)}, u32[]{:S(2)}, u32[]{:S(2)}) collective-permute-start(f32[1,2,1,120,512]{4,3,0,1,2:T(8,128)} %copy.74), channel_id=1, source_target_pairs={{128,0},{0,128},{129,1},{1,129},{130,2},{2,130},{131,3},{3,131},{1... | collective-permute-start | bytes 1474568 | tf_op jit(solution)/shard_map/ppermute | solution.py:17
  13.5 12.3 %collective-permute-start = (f32[1,2,1,120,512]{4,3,0,1,2:T(8,128)}, f32[1,2,1,120,512]{4,3,0,1,2:T(8,128)}, u32[]{:S(2)}, u32[]{:S(2)}) collective-permute-start(f32[1,2,1,120,512]{4,3,0,1,2:T(8,128)} %copy.75), channel_id=1, source_target_pairs={{0,128},{128,0},{1,129},{129,1},{2,130},{130,2},{3,131},{131,3},{4... | collective-permute-start | bytes 1474568 | tf_op jit(solution)/shard_map/ppermute | solution.py:16
  25.6 1.4 copy-start.6
  28.7 1.0 copy-start.9
  29.3 1.9 copy-start.2
  31.2 155.3 %copy-start.10 = (f32[1,1,16,512]{3,2,1,0:T(8,128)S(1)}, f32[1,1,16,512]{3,2,1,0:T(8,128)}, u32[]{:S(2)}) copy-start(f32[1,1,16,512]{3,2,1,0:T(8,128)} %param.20) | copy-start | bytes 98308
  32.9 305.4 %all-reduce.6.cloned.1.call-start = ((), (), s32[]{:S(2)}) async-start(), calls=%async_computation.1 | async-start | bytes 2097152 | tf_op jit(solution)/shard_map/psum | solution.py:83
  33.0 305.6 %copy-start.11 = (f32[1,1,16,512]{3,2,1,0:T(8,128)S(1)}, f32[1,1,16,512]{3,2,1,0:T(8,128)}, u32[]{:S(2)}) copy-start(f32[1,1,16,512]{3,2,1,0:T(8,128)} %param.19) | copy-start | bytes 98308
  186.5 152.0 %copy-start.8 = (f32[512,512]{1,0:T(8,128)S(1)}, f32[512,512]{1,0:T(8,128)}, u32[]{:S(2)}) copy-start(f32[512,512]{1,0:T(8,128)} %all-reduce.4.cloned.1.call-done) | copy-start | bytes 3145732
  189.4 213.9 %all-reduce.8.cloned.1.call-start = ((), (), s32[]{:S(2)}) async-start(), calls=%async_computation.2 | async-start | bytes 2097152 | tf_op jit(solution)/shard_map/psum | solution.py:84
  338.3 148.3 %all-gather.2.cloned.1.call-start = ((), (), s32[]{:S(2)}) async-start(), calls=%async_computation.3 | async-start | bytes 1081344 | tf_op jit(solution)/shard_map/all_gather | solution.py:87
  488.5 2.1 copy-start.3
  492.5 3.3 collective-permute-start.5
  492.6 3.2 collective-permute-start.4
  493.7 13.3 %collective-permute-start.6 = (f32[2,1,1,120,512]{4,3,0,2,1:T(8,128)S(1)}, f32[2,1,1,120,512]{4,3,0,2,1:T(8,128)S(1)}, u32[]{:S(2)}, u32[]{:S(2)}) collective-permute-start(f32[2,1,1,120,512]{4,3,0,2,1:T(8,128)S(1)} %get-tuple-element.27), channel_id=1, source_target_pairs={{0,32},{32,64},{64,96},{96,0},{1,33},{33,65},{65,97},{97,1},{2,34}... | collective-permute-start | bytes 1474568 | tf_op jit(solution)/shard_map/ppermute | solution.py:16
  494.4 14.2 %collective-permute-start.7 = (f32[2,1,1,120,512]{4,3,0,2,1:T(8,128)S(1)}, f32[2,1,1,120,512]{4,3,0,2,1:T(8,128)S(1)}, u32[]{:S(2)}, u32[]{:S(2)}) collective-permute-start(f32[2,1,1,120,512]{4,3,0,2,1:T(8,128)S(1)} %get-tuple-element.28), channel_id=1, source_target_pairs={{32,0},{64,32},{96,64},{0,96},{33,1},{65,33},{97,65},{1,97},{34,2}... | collective-permute-start | bytes 1474568 | tf_op jit(solution)/shard_map/ppermute | solution.py:17
  509.7 1.5 copy-start.7
  513.8 2.1 copy-start.1
Sparse Core Ops, SparseCore 0:
  33.0 153.4 all-reduce.3
  190.5 147.6 all-reduce.5
  340.6 62.6 all-reduce.7
  408.4 78.0 all-gather.1
where the time goes:
time: 523 us; the launch traced here: 522 us
  waiting for transfers between devices  464 us (89%)
  matrix products  17.2 us (3%)
  between operations  14.1 us (3%)
  local copies, waits for them, and re-layouts  13.3 us (3%)
  other arithmetic  8.02 us (2%)
  starting transfers between devices  5.73 us (1%)
    psum x1, waiting for transfers between devices, on_device(): column_res = lax.psum(column_part, 'gz')  154 us
    psum x1, waiting for transfers between devices, on_device(): column_top = lax.psum(top_part, 'gz')  149 us
    all_gather x1, waiting for transfers between devices, on_device(): column_vals = lax.all_gather(value_rows, 'gz', axis=0, tiled=True)  78.2 us
    psum x1, waiting for transfers between devices, on_device(): top_res = lax.psum(column_top, ('gx', 'gy'))  64.1 us
    ppermute x4, waiting for transfers between devices, with_halo(): before = lax.ppermute(last, axis, up)  16.6 us
  transfers between devices with their start and end apart: 12, of which 8 were waited for; matrix products, arithmetic and copies ran while one was open for 2% of the time, Pallas kernels for 0%

commit v1 on v0

--- a/solution.py
+++ b/solution.py
@@ -81,7 +81,8 @@
     level_two = jnp.dot(inverse_rows, column_res, precision=high)
     top_part = lax.dot_general(basis_rows, own_rows, (((0,), (0,)), ((), ())), precision=high)
     column_top = lax.psum(top_part, "gz")
-    top_res = lax.psum(column_top, ("gx", "gy"))
+    one_axis = lax.psum(column_top, "gx")
+    top_res = lax.psum(one_axis, "gy")
     level_three = jnp.dot(top_inverse, top_res, precision=high)
     value_rows = level_two + jnp.dot(basis_rows, level_three, precision=high)
     column_vals = lax.all_gather(value_rows, "gz", axis=0, tiled=True)

time: 523 us -> 542 us (1.036)
  waiting for transfers between devices: 464 us -> 483 us
    psum x1 -> x2, waiting for transfers between devices: 64.1 us -> 83.1 us  [the longest x1 53.1 us: on_device(): top_res = lax.psum(one_axis, 'gy')]
  transfers between devices with their start and end apart: 12 -> 13, of which waited for: 8 -> 9; matrix products, arithmetic and copies ran while one was open for 2% -> 2% of each run, Pallas kernels for 0% -> 0%
where the time goes in v1:
time: 542 us; the launch traced here: 541 us
  waiting for transfers between devices  483 us (89%)
  matrix products  17.2 us (3%)
  between operations  14.1 us (3%)
  local copies, waits for them, and re-layouts  13.3 us (2%)
  other arithmetic  8.02 us (1%)
  starting transfers between devices  5.77 us (1%)
    psum x1, waiting for transfers between devices, on_device(): column_res = lax.psum(column_part, 'gz')  154 us
    psum x1, waiting for transfers between devices, on_device(): column_top = lax.psum(top_part, 'gz')  149 us
    all_gather x1, waiting for transfers between devices, on_device(): column_vals = lax.all_gather(value_rows, 'gz', axis=0, tiled=True)  78.1 us
    psum x1, waiting for transfers between devices, on_device(): top_res = lax.psum(one_axis, 'gy')  53.1 us
    psum x1, waiting for transfers between devices, on_device(): one_axis = lax.psum(column_top, 'gx')  30 us
    ppermute x4, waiting for transfers between devices, with_halo(): before = lax.ppermute(last, axis, up)  16.6 us
  transfers between devices with their start and end apart: 13, of which 9 were waited for; matrix products, arithmetic and copies ran while one was open for 2% of the time, Pallas kernels for 0%

profile of v1, /device:TPU:6, one launch (start us, length us, event | category | flops | bytes accessed | tf_op | source)
XLA Modules:
  0.0 541.4 jit_solution(12656897857102789408)
XLA Ops:
  7.2 2.4 fusion.25
  9.6 2.2 collective-permute-start.2
  11.9 0.8 copy.74
  12.7 0.8 copy.75
  13.5 0.5 collective-permute-start
  14.0 0.6 broadcast.80
  14.6 0.6 reduce.3
  15.8 7.1 %collective-permute-done.2 = f32[2,1,1,120,512]{4,3,1,0,2:T(8,128)} collective-permute-done((f32[2,1,1,120,512]{4,3,1,0,2:T(8,128)}, f32[2,1,1,120,512]{4,3,1,0,2:T(8,128)}, u32[]{:S(2)}, u32[]{:S(2)}) %collective-permute-start.2) | collective-permute-done | bytes 491552 | tf_op jit(solution)/shard_map/ppermute | solution.py:16
  22.9 1.2 collective-permute-done.3
  24.1 1.5 fusion.3
  25.6 0.2 slice_bitcast_fusion.3
  25.9 1.1 copy-done.6
  27.0 1.5 maximum_add_fusion
  28.7 0.6 pad_maximum_fusion
  29.3 0.3 copy-done.9
  29.7 0.5 fusion.7
  30.2 1.0 copy-done.2
  31.2 1.7 fusion.8
  33.0 153.6 %all-reduce.5.cloned.1.call-done = f32[512,512]{1,0:T(8,128)} async-done(((f32[512,512]{1,0:T(8,128)}), f32[512,512]{1,0:T(8,128)}) %all-reduce.5.cloned.1.call-update) | async-done | bytes 1048592 | tf_op jit(solution)/shard_map/psum | solution.py:75
  186.5 2.8 convolution_bitcast_fusion
  189.4 148.9 %all-reduce.7.cloned.1.call-done = f32[512,512]{0,1:T(8,128)} async-done(((f32[512,512]{0,1:T(8,128)}), f32[512,512]{0,1:T(8,128)}) %all-reduce.7.cloned.1.call-update) | async-done | bytes 1048592 | tf_op jit(solution)/shard_map/psum | solution.py:83
  338.3 30.0 %all-reduce.9.cloned.1.call-done = f32[512,512]{0,1:T(8,128)} async-done(((f32[512,512]{0,1:T(8,128)}), f32[512,512]{0,1:T(8,128)}) %all-reduce.9.cloned.1.call-update) | async-done | bytes 1048592 | tf_op jit(solution)/shard_map/psum | solution.py:84
  368.6 0.7 fusion.15
  369.2 53.1 %all-reduce.11.cloned.1.call-done = f32[512,512]{0,1:T(8,128)} async-done(((f32[512,512]{0,1:T(8,128)}), f32[512,512]{0,1:T(8,128)}) %all-reduce.11.cloned.1.call-update) | async-done | bytes 1048592 | tf_op jit(solution)/shard_map/psum | solution.py:85
  422.3 3.4 fusion.26
  425.7 1.6 fusion.5
  427.5 78.1 %all-gather.2.cloned.1.call-done = f32[512,512]{1,0:T(8,128)} async-done(((f32[16,512]{1,0:T(8,128)}), f32[512,512]{1,0:T(8,128)}) %all-gather.2.cloned.1.call-update) | async-done | bytes 1048592 | tf_op jit(solution)/shard_map/all_gather | solution.py:88
  505.6 1.9 convolution_convert_fusion
  507.6 0.7 fusion.27
  508.3 1.4 copy-done.3
  509.7 1.3 convolution_add_fusion
  511.0 0.3 copy_multiply_fusion
  511.6 0.5 collective-permute-start.4
  512.1 0.4 slice_bitcast_fusion.6
  512.8 0.6 collective-permute-start.6
  513.4 1.5 collective-permute-start.7
  514.9 0.3 maximum_add_fusion.2
  515.2 1.3 copy.68
  516.6 9.4 %collective-permute-done.6 = f32[2,1,1,120,512]{4,3,0,2,1:T(8,128)S(1)} collective-permute-done((f32[2,1,1,120,512]{4,3,0,2,1:T(8,128)S(1)}, f32[2,1,1,120,512]{4,3,0,2,1:T(8,128)S(1)}, u32[]{:S(2)}, u32[]{:S(2)}) %collective-permute-start.6) | collective-permute-done | bytes 491552 | tf_op jit(solution)/shard_map/ppermute | solution.py:16
  526.1 1.5 collective-permute-done.7
  527.6 0.3 maximum_add_fusion.4
  527.9 0.2 slice_bitcast_fusion.1
  528.2 0.6 pad_maximum_fusion.1
  528.8 0.6 copy.67
  529.3 1.0 copy-done.7
  530.3 2.5 fusion.2
  532.8 1.5 fusion.4
  534.3 0.6 copy-done.1
  (59 shorter events, 2.0 us)
Async XLA Ops:
  7.2 501.1 %copy-start = (bf16[2,2,1,480,480]{4,3,2,1,0:T(8,128)(2,1)S(1)}, bf16[2,2,1,480,480]{4,3,2,1,0:T(8,128)(2,1)}, u32[]{:S(2)}) copy-start(bf16[2,2,1,480,480]{4,3,2,1,0:T(8,128)(2,1)} %param.15) | copy-start | bytes 5529604
  7.2 4.6 copy-start.5
  7.2 179.3 %all-reduce.5.cloned.1.call-start = ((), (), s32[]{:S(2)}) async-start(), calls=%async_computation | async-start | bytes 2097152 | tf_op jit(solution)/shard_map/psum | solution.py:75
  9.6 13.3 %collective-permute-start.2 = (f32[2,1,1,120,512]{4,3,1,0,2:T(8,128)}, f32[2,1,1,120,512]{4,3,1,0,2:T(8,128)}, u32[]{:S(2)}, u32[]{:S(2)}) collective-permute-start(f32[2,1,1,120,512]{4,3,1,0,2:T(8,128)} %get-tuple-element.35), channel_id=1, source_target_pairs={{0,32},{32,64},{64,96},{96,0},{1,33},{33,65},{65,97},{97,1},{2,34}... | collective-permute-start | bytes 1474568 | tf_op jit(solution)/shard_map/ppermute | solution.py:16
  11.8 12.3 %collective-permute-start.3 = (f32[2,1,1,120,512]{4,3,1,0,2:T(8,128)}, f32[2,1,1,120,512]{4,3,1,0,2:T(8,128)}, u32[]{:S(2)}, u32[]{:S(2)}) collective-permute-start(f32[2,1,1,120,512]{4,3,1,0,2:T(8,128)} %get-tuple-element.36), channel_id=1, source_target_pairs={{32,0},{64,32},{96,64},{0,96},{33,1},{65,33},{97,65},{1,97},{34,2}... | collective-permute-start | bytes 1474568 | tf_op jit(solution)/shard_map/ppermute | solution.py:17
  11.9 2.2 copy-start.13
  11.9 2.7 copy-start.14
  11.9 3.7 copy-start.12
  11.9 12.2 %copy-start.4 = (f32[2,3,1,120,512]{4,3,2,1,0:T(8,128)S(1)}, f32[2,3,1,120,512]{4,3,2,1,0:T(8,128)}, u32[]{:S(2)}) copy-start(f32[2,3,1,120,512]{4,3,2,1,0:T(8,128)} %param.12) | copy-start | bytes 4423684
  12.7 13.1 %collective-permute-start.1 = (f32[1,2,1,120,512]{4,3,0,1,2:T(8,128)}, f32[1,2,1,120,512]{4,3,0,1,2:T(8,128)}, u32[]{:S(2)}, u32[]{:S(2)}) collective-permute-start(f32[1,2,1,120,512]{4,3,0,1,2:T(8,128)} %copy.74), channel_id=1, source_target_pairs={{128,0},{0,128},{129,1},{1,129},{130,2},{2,130},{131,3},{3,131},{1... | collective-permute-start | bytes 1474568 | tf_op jit(solution)/shard_map/ppermute | solution.py:17
  13.5 12.3 %collective-permute-start = (f32[1,2,1,120,512]{4,3,0,1,2:T(8,128)}, f32[1,2,1,120,512]{4,3,0,1,2:T(8,128)}, u32[]{:S(2)}, u32[]{:S(2)}) collective-permute-start(f32[1,2,1,120,512]{4,3,0,1,2:T(8,128)} %copy.75), channel_id=1, source_target_pairs={{0,128},{128,0},{1,129},{129,1},{2,130},{130,2},{3,131},{131,3},{4... | collective-permute-start | bytes 1474568 | tf_op jit(solution)/shard_map/ppermute | solution.py:16
  25.6 1.4 copy-start.6
  28.7 1.0 copy-start.9
  29.3 1.9 copy-start.2
  31.2 155.3 %copy-start.10 = (f32[1,1,16,512]{3,2,1,0:T(8,128)S(1)}, f32[1,1,16,512]{3,2,1,0:T(8,128)}, u32[]{:S(2)}) copy-start(f32[1,1,16,512]{3,2,1,0:T(8,128)} %param.20) | copy-start | bytes 98308
  32.9 305.4 %all-reduce.7.cloned.1.call-start = ((), (), s32[]{:S(2)}) async-start(), calls=%async_computation.1 | async-start | bytes 2097152 | tf_op jit(solution)/shard_map/psum | solution.py:83
  189.3 179.3 %copy-start.8 = (f32[512,512]{1,0:T(8,128)S(1)}, f32[512,512]{1,0:T(8,128)}, u32[]{:S(2)}) copy-start(f32[512,512]{1,0:T(8,128)} %all-reduce.5.cloned.1.call-done) | copy-start | bytes 3145732
  189.3 179.3 %copy-start.11 = (f32[1,1,16,512]{3,2,1,0:T(8,128)S(1)}, f32[1,1,16,512]{3,2,1,0:T(8,128)}, u32[]{:S(2)}) copy-start(f32[1,1,16,512]{3,2,1,0:T(8,128)} %param.19) | copy-start | bytes 98308
  189.3 179.0 %all-reduce.9.cloned.1.call-start = ((), (), s32[]{:S(2)}) async-start(), calls=%async_computation.2 | async-start | bytes 2097152 | tf_op jit(solution)/shard_map/psum | solution.py:84
  338.3 84.1 %all-reduce.11.cloned.1.call-start = ((), (), s32[]{:S(2)}) async-start(), calls=%async_computation.3 | async-start | bytes 2097152 | tf_op jit(solution)/shard_map/psum | solution.py:85
  368.3 137.3 %all-gather.2.cloned.1.call-start = ((), (), s32[]{:S(2)}) async-start(), calls=%async_computation.4 | async-start | bytes 1081344 | tf_op jit(solution)/shard_map/all_gather | solution.py:88
  507.6 2.1 copy-start.3
  511.5 3.3 collective-permute-start.5
  511.6 3.2 collective-permute-start.4
  512.8 13.3 %collective-permute-start.6 = (f32[2,1,1,120,512]{4,3,0,2,1:T(8,128)S(1)}, f32[2,1,1,120,512]{4,3,0,2,1:T(8,128)S(1)}, u32[]{:S(2)}, u32[]{:S(2)}) collective-permute-start(f32[2,1,1,120,512]{4,3,0,2,1:T(8,128)S(1)} %get-tuple-element.27), channel_id=1, source_target_pairs={{0,32},{32,64},{64,96},{96,0},{1,33},{33,65},{65,97},{97,1},{2,34}... | collective-permute-start | bytes 1474568 | tf_op jit(solution)/shard_map/ppermute | solution.py:16
  513.4 14.2 %collective-permute-start.7 = (f32[2,1,1,120,512]{4,3,0,2,1:T(8,128)S(1)}, f32[2,1,1,120,512]{4,3,0,2,1:T(8,128)S(1)}, u32[]{:S(2)}, u32[]{:S(2)}) collective-permute-start(f32[2,1,1,120,512]{4,3,0,2,1:T(8,128)S(1)} %get-tuple-element.28), channel_id=1, source_target_pairs={{32,0},{64,32},{96,64},{0,96},{33,1},{65,33},{97,65},{1,97},{34,2}... | collective-permute-start | bytes 1474568 | tf_op jit(solution)/shard_map/ppermute | solution.py:17
  528.7 1.5 copy-start.7
  532.8 2.1 copy-start.1
Sparse Core Ops, SparseCore 0:
  33.0 153.4 all-reduce.4
  190.5 147.6 all-reduce.6
  340.9 27.3 all-reduce.8
  370.5 51.7 all-reduce.10
  427.5 78.0 all-gather.1
